TPU v7x, 32 devices: a whole 2x2x4 slice. The times are simulated.
32 devices in a mesh: cuts: 2 (over y), idx: 8 (over z, x), half: 2 (over core).
Axes of the slice: x: 2, y: 2, z: 4, core: 2. Of those that a mesh axis runs over, the one named last changes fastest.
Arguments:
- left_factor: float32 [2, 4, 64, 1024, 256], P('half', 'cuts', 'idx'), parts along dimension 1, may hold values from -6 to 6
- right_factor: float32 [2, 4, 64, 256, 1024], P('half', 'cuts', None, 'idx'), parts along dimension 1, may hold values from -0.25 to 0.25
Outputs:
- amplitudes: float32 [1024, 4, 1024], P(('idx', 'half'), 'cuts'), parts along dimension 1
There are 2 independent parts, one for each index of `cuts`. A program takes and returns all parts, laid end to end along the dimension named above; each array names one. Nothing has to cross between parts.
All inputs are finite; a program needn't handle non-finite values.
Results may differ from a plain program's by a relative error of at most 0.0003.
Values sent between devices are 32-bit elements; how exact they have to be, the bound alone decides.
A program may use at most 256 MiB of HBM per device.

v0:
```python
import math
import jax
import jax.numpy as jnp
from jax import lax
from jax.sharding import PartitionSpec as P

HIGH = lax.Precision.HIGH
CHUNKS = (3, 1)


def swapped(x, axis, bit):
    return lax.ppermute(x, axis, [(i, i ^ 1 << bit) for i in range(lax.axis_size(axis))])


def complex_product(left_real, left_imag, right_real, right_imag, pattern):
    first_term = jnp.einsum(pattern, left_real, right_real, precision=HIGH)
    second_term = jnp.einsum(pattern, left_imag, right_imag, precision=HIGH)
    mixed_term = jnp.einsum(pattern, left_real + left_imag, right_real + right_imag, precision=HIGH)
    return (first_term - second_term, mixed_term - first_term - second_term)


def by_columns(left_local, right_local, norm_scale):
    columns = lax.all_to_all(right_local, "idx", split_axis=1, concat_axis=2, tiled=True)
    merged = jnp.stack(
        complex_product(left_local[0], left_local[1], columns[0], columns[1], "bmk,bkn->bmn")
    )
    half_cols = merged.shape[3] // 2
    half_index = lax.axis_index("half")
    outgoing = lax.dynamic_slice_in_dim(merged, (1 - half_index) * half_cols, half_cols, 3)
    own_slab = lax.dynamic_slice_in_dim(merged, half_index * half_cols, half_cols, 3)
    other_slab = swapped(outgoing, "half", 0)
    is_lower = half_index == 0
    first_pair = jnp.where(is_lower, own_slab, other_slab)
    second_pair = jnp.where(is_lower, other_slab, own_slab)
    real_part, imag_part = complex_product(
        first_pair[0], first_pair[1], second_pair[0], second_pair[1], "bmn,bon->mo"
    )
    return jnp.stack([real_part, imag_part], axis=1) * norm_scale


def by_batch(left_local, right_local, norm_scale):
    idx, half = (lax.axis_size("idx"), lax.axis_size("half"))
    planes, batch, rows, between = right_local.shape
    mine = left_local.shape[1] // half
    half_index = lax.axis_index("half")
    blocks = right_local.reshape(planes, idx * half, mine, rows, between)
    sizes = CHUNKS if sum(CHUNKS) == mine else (mine,)
    received = []
    start = 0
    for size in sizes:
        piece = blocks[:, :, start : start + size].transpose(1, 0, 2, 3, 4)
        received.append(
            lax.all_to_all(piece, ("idx", "half"), split_axis=0, concat_axis=0, tiled=True)
        )
        start += size
    outgoing = lax.dynamic_slice_in_dim(left_local, (1 - half_index) * mine, mine, 1)
    own = lax.dynamic_slice_in_dim(left_local, half_index * mine, mine, 1)
    other = swapped(outgoing, "half", 0)
    is_lower = half_index == 0
    first = jnp.where(is_lower, own, other)
    second = jnp.where(is_lower, other, own)
    total = None
    start = 0
    for size, got in zip(sizes, received):
        got = got.reshape(idx, half, planes, size, rows, between)
        pairs = got.transpose(1, 2, 3, 0, 4, 5).reshape(half, planes, size, idx * rows, between)
        inner = complex_product(pairs[0, 0], pairs[0, 1], pairs[1, 0], pairs[1, 1], "bkn,bln->bkl")
        a = first[:, start : start + size]
        b = second[:, start : start + size]
        partial = complex_product(a[0], a[1], inner[0], inner[1], "bmk,bkl->bml")
        term = complex_product(partial[0], partial[1], b[0], b[1], "bml,bol->mo")
        total = term if total is None else (total[0] + term[0], total[1] + term[1])
        start += size
    return jnp.stack(total, axis=1) * norm_scale


def on_device(left_factor, right_factor):
    left_local = left_factor[0]
    right_local = right_factor[0]
    batch, between = (right_local.shape[1], right_local.shape[3])
    norm_scale = 1.0 / math.sqrt(2.0 * batch * between)
    shared = left_local.shape[1] % lax.axis_size("half") == 0
    form = by_batch if shared else by_columns
    return lax.psum_scatter(
        form(left_local, right_local, norm_scale), ("idx", "half"), scatter_dimension=0, tiled=True
    )


def solution(mesh):
    return jax.shard_map(
        on_device,
        mesh=mesh,
        in_specs=(P("half", "cuts", "idx", None, None), P("half", "cuts", None, "idx", None)),
        out_specs=P(("idx", "half"), "cuts", None),
        check_vma=False,
    )
```

profile of v0, /device:TPU:0, one launch (start us, length us, event | category | flops | bytes accessed | tf_op | source)
XLA Modules:
  0.0 577.8 jit_solution(6922426632892912840)
XLA Ops:
  6.5 2.5 slice_bitcast_fusion.1
  11.3 7.4 %all-to-all-start.1 = ((f32[16,2,1,32,1024]{4,3,2,1,0:T(8,128)}), f32[16,2,1,32,1024]{4,3,2,1,0:T(8,128)}, u32[]{:S(2)}, u32[]{:S(2)}) async-start(f32[16,2,1,32,1024]{4,3,2,1,0:T(8,128)} %copy.17), calls=%async_computation.1 | async-start | bytes 8388608 | tf_op jit(solution)/shard_map/all_to_all | solution.py:53
  18.8 11.8 %slice_bitcast_fusion = f32[16,2,3,32,1024]{4,3,2,0,1:T(8,128)} fusion(f32[2,16,4,32,1024]{4,3,2,1,0:T(8,128)} %bitcast.163), kind=kLoop, calls=%fused_computation | loop fusion | bytes 25165824 | tf_op jit(solution)/shard_map/transpose | solution.py:51
  30.6 11.8 %copy.15 = f32[16,2,3,32,1024]{4,3,2,1,0:T(8,128)} copy(f32[16,2,3,32,1024]{4,3,2,0,1:T(8,128)} %slice_bitcast_fusion) | data formatting | bytes 25165824 | tf_op jit(solution)/shard_map/transpose | solution.py:51
  42.4 53.9 %all-to-all-done.1 = f32[16,2,1,32,1024]{4,3,2,1,0:T(8,128)} async-done(((f32[16,2,1,32,1024]{4,3,2,1,0:T(8,128)}), f32[16,2,1,32,1024]{4,3,2,1,0:T(8,128)}, u32[]{:S(2)}, u32[]{:S(2)}) %all-to-all-start.1) | async-done | bytes 4194336 | tf_op jit(solution)/shard_map/all_to_all | solution.py:53
  96.3 19.7 %all-to-all-start = ((f32[16,2,3,32,1024]{4,3,2,1,0:T(8,128)}), f32[16,2,3,32,1024]{4,3,2,1,0:T(8,128)}, u32[]{:S(2)}, u32[]{:S(2)}) async-start(f32[16,2,3,32,1024]{4,3,2,1,0:T(8,128)} %copy.15), calls=%async_computation | async-start | bytes 25165824 | tf_op jit(solution)/shard_map/all_to_all | solution.py:53
  116.1 7.2 %dynamic-slice_bitcast_fusion = f32[2,4,1024,256]{3,2,1,0:T(8,128)} fusion(f32[1,2,8,1024,256]{4,3,2,1,0:T(8,128)} %param.2, s32[]{:T(128)S(6)} %select_n.20), kind=kLoop, calls=%fused_computation.4 | loop fusion | bytes 16777220 | tf_op jit(solution)/shard_map/dynamic_slice | solution.py:56
  128.0 8.7 %collective-permute-done = f32[2,4,1024,256]{3,2,1,0:T(8,128)} collective-permute-done((f32[2,4,1024,256]{3,2,1,0:T(8,128)}, f32[2,4,1024,256]{3,2,1,0:T(8,128)}, u32[]{:S(2)}, u32[]{:S(2)}) %collective-permute-start) | collective-permute-done | bytes 8388640 | tf_op jit(solution)/shard_map/ppermute | solution.py:12
  136.7 7.0 %bitcast_select_fusion = (f32[2,4,1024,256]{3,2,1,0:T(8,128)S(1)}, f32[2,4,1024,256]{3,2,1,0:T(8,128)S(1)}) fusion(f32[2,4,1024,256]{3,2,1,0:T(8,128)} %collective-permute-done, f32[1,2,8,1024,256]{4,3,2,1,0:T(8,128)} %param.2, s32[]{:T(128)S(6)} %select_n.19, pred[]{:T(512)S(6)} %eq.3), kind=kLoop, calls=%fused_computation.2 | loop fusion | flops 4194304 | bytes 33554436 | tf_op jit(solution)/shard_map/jit(_where)/select_n | solution.py:61
  147.0 3.8 fusion.41
  150.8 3.9 fusion.44
  154.7 3.8 fusion.39
  158.5 181.1 %all-to-all-done = f32[16,2,3,32,1024]{4,3,2,1,0:T(8,128)} async-done(((f32[16,2,3,32,1024]{4,3,2,1,0:T(8,128)}), f32[16,2,3,32,1024]{4,3,2,1,0:T(8,128)}, u32[]{:S(2)}, u32[]{:S(2)}) %all-to-all-start) | async-done | bytes 12582944 | tf_op jit(solution)/shard_map/all_to_all | solution.py:53
  339.6 11.8 %copy.16 = f32[2,2,3,8,32,1024]{5,4,3,2,1,0:T(8,128)} copy(f32[2,2,3,8,32,1024]{5,4,2,1,0,3:T(8,128)} %bitcast.6) | data formatting | bytes 25165824 | tf_op jit(solution)/shard_map/transpose | solution.py:66
  351.5 4.6 fusion.15
  356.0 5.4 fusion.14
  363.2 3.4 fusion.13
  368.2 3.5 subtract_subtract_fusion
  371.7 6.9 %fusion.17 = f32[1024,1024,1]{1,0,2:T(8,128)} fusion(f32[2,4,1024,256]{3,2,1,0:T(8,128)S(1)} %bitcast.158, f32[3,1024,256]{2,1,0:T(8,128)S(1)} %fusion.13, f32[3,1024,256]{2,1,0:T(8,128)S(1)} %fusion.16), kind=kOutput, calls=%fused_computation.34 | convolution fusion | flops 4832624640 | bytes 13631488 | tf_op jit(solution)/shard_map/bml,bol->mo/dot_general | solution.py:16
  378.6 6.9 %fusion.18 = f32[1024,1024,1]{1,0,2:T(8,128)} fusion(f32[3,1024,256]{2,1,0:T(8,128)S(1)} %copy-done.4, f32[2,4,1024,256]{3,2,1,0:T(8,128)S(1)} %bitcast.158), kind=kOutput, calls=%fused_computation.35 | convolution fusion | flops 4831838208 | bytes 10485760 | tf_op jit(solution)/shard_map/bml,bol->mo/dot_general | solution.py:17
  385.5 8.7 %fusion.4 = f32[1024,1,1024]{2,0,1:T(8,128)} fusion(f32[1024,1024,1]{1,0,2:T(8,128)} %fusion.18, f32[1024,1024,1]{1,0,2:T(8,128)} %fusion.17, f32[1024,1024]{1,0:T(8,128)S(1)} %copy-done.3, f32[1024,1024]{1,0:T(8,128)} %fusion.41), kind=kLoop, calls=%fused_computation.12 | loop fusion | flops 3145728 | bytes 20971520 | tf_op jit(solution)/shard_map/stack | solution.py:74
  394.2 13.3 %fusion.2 = f32[1024,1,1024]{2,0,1:T(8,128)} fusion(f32[1024,1024,1]{1,0,2:T(8,128)} %fusion.18, f32[1024,1024,1]{1,0,2:T(8,128)} %fusion.17, f32[1024,1024]{1,0:T(8,128)} %fusion.41, f32[1024,1024]{1,0:T(8,128)} %fusion.39, f32[1024,1024]{1,0:T(8,128)S(1)} %copy-done.3, f32[2,4,1024,256]{3,2,1,0:T(8,128)} %copy-done.2, ...), kind=kOutput, calls=%fused_computation.9 | convolution fusion | flops 4839440384 | bytes 40894464 | tf_op jit(solution)/shard_map/bml,bol->mo/dot_general | solution.py:18
  407.5 8.7 %maximum_multiply_fusion = f32[1024,2,1024]{2,0,1:T(8,128)} fusion(f32[1024,1,1024]{2,0,1:T(8,128)} %fusion.2, f32[1024,1,1024]{2,0,1:T(8,128)} %fusion.4), kind=kLoop, calls=%fused_computation.1 | loop fusion | flops 4194304 | bytes 16777216 | tf_op jit(solution)/shard_map/mul | solution.py:74
  416.2 152.3 %reduce-scatter.2.cloned.1.call-done = f32[64,2,1024]{2,0,1:T(8,128)} async-done(((f32[1024,2,1024]{2,0,1:T(8,128)}), f32[64,2,1024]{2,0,1:T(8,128)}) %reduce-scatter.2.cloned.1.call-update) | async-done | bytes 524304 | tf_op jit(solution)/shard_map/reduce_scatter | solution.py:84
  (34 shorter events, 15.9 us)
Async XLA Ops:
  11.3 85.0 %all-to-all-start.1 = ((f32[16,2,1,32,1024]{4,3,2,1,0:T(8,128)}), f32[16,2,1,32,1024]{4,3,2,1,0:T(8,128)}, u32[]{:S(2)}, u32[]{:S(2)}) async-start(f32[16,2,1,32,1024]{4,3,2,1,0:T(8,128)} %copy.17), calls=%async_computation.1 | async-start | bytes 8388608 | tf_op jit(solution)/shard_map/all_to_all | solution.py:53
  96.3 243.3 %all-to-all-start = ((f32[16,2,3,32,1024]{4,3,2,1,0:T(8,128)}), f32[16,2,3,32,1024]{4,3,2,1,0:T(8,128)}, u32[]{:S(2)}, u32[]{:S(2)}) async-start(f32[16,2,3,32,1024]{4,3,2,1,0:T(8,128)} %copy.15), calls=%async_computation | async-start | bytes 25165824 | tf_op jit(solution)/shard_map/all_to_all | solution.py:53
  116.0 452.5 %reduce-scatter.2.cloned.1.call-start = ((), (), s32[]{:S(2)}) async-start(), calls=%async_computation.3 | async-start | bytes 8912896 | tf_op jit(solution)/shard_map/reduce_scatter | solution.py:84
  123.2 13.5 %collective-permute-start = (f32[2,4,1024,256]{3,2,1,0:T(8,128)}, f32[2,4,1024,256]{3,2,1,0:T(8,128)}, u32[]{:S(2)}, u32[]{:S(2)}) collective-permute-start(f32[2,4,1024,256]{3,2,1,0:T(8,128)} %dynamic-slice_bitcast_fusion), channel_id=1, source_target_pairs={{0,1},{1,0},{2,3},{3,2},{4,5},{5,4},{6,7},{7,6},{8,9},{9,8},{10,11... | collective-permute-start | bytes 25165832 | tf_op jit(solution)/shard_map/ppermute | solution.py:12
  143.7 3.2 copy-start.1
  143.8 10.9 %copy-start.2 = (f32[2,4,1024,256]{3,2,1,0:T(8,128)}, f32[2,4,1024,256]{3,2,1,0:T(8,128)S(1)}, u32[]{:S(2)}) copy-start(f32[2,4,1024,256]{3,2,1,0:T(8,128)S(1)} %get-tuple-element.5) | copy-start | bytes 25165828
  351.5 9.9 %copy-start = (f32[2,2,3,8,32,1024]{5,4,3,2,1,0:T(8,128)S(1)}, f32[2,2,3,8,32,1024]{5,4,3,2,1,0:T(8,128)}, u32[]{:S(2)}) copy-start(f32[2,2,3,8,32,1024]{5,4,3,2,1,0:T(8,128)} %copy.16) | copy-start | bytes 37748740
  356.0 10.6 %slice-start = ((s8[8388608]{0:T(1024)(128)(4,1)}), s8[4194304]{0:T(1024)(128)(4,1)S(1)}, s32[]{:S(2)}) async-start(s8[8388608]{0:T(1024)(128)(4,1)} %bitcast.155), calls=%async_computation.4 | async-start | bytes 8388608
  361.4 5.2 slice-start.1
  366.7 5.1 slice-start.2
  368.2 3.5 slice-start.3
  371.7 6.9 %copy-start.4 = (f32[3,1024,256]{2,1,0:T(8,128)S(1)}, f32[3,1024,256]{2,1,0:T(8,128)}, u32[]{:S(2)}) copy-start(f32[3,1024,256]{2,1,0:T(8,128)} %subtract_subtract_fusion) | copy-start | bytes 9437188
  378.6 6.9 %copy-start.3 = (f32[1024,1024]{1,0:T(8,128)S(1)}, f32[1024,1024]{1,0:T(8,128)}, u32[]{:S(2)}) copy-start(f32[1024,1024]{1,0:T(8,128)} %fusion.44) | copy-start | bytes 12582916
Sparse Core Ops, SparseCore 0:
  416.4 152.1 reduce-scatter.1
where the time goes:
time: 584 us; the launch traced here: 578 us
  waiting for transfers between devices  396 us (68%)
  matrix products  62.4 us (11%)
  local copies, waits for them, and re-layouts  53.6 us (9%)
  starting transfers between devices  27.5 us (5%)
  other arithmetic  24.4 us (4%)
  between operations  13.9 us (2%)
    all_to_all x2, waiting for transfers between devices, by_batch(): lax.all_to_all(piece, ('idx', 'half'), split_axis=0, concat_axis=0, tiled...  235 us
    reduce_scatter x1, waiting for transfers between devices, on_device(): lax.psum_scatter(form(left_local, right_local, norm_scale), ('idx', 'half...  152 us
    transpose x4, local copies, waits for them, and re-layouts, by_batch(): piece = blocks[:, :, start:start + size].transpose(1, 0, 2, 3, 4)  28.4 us
    all_to_all x2, starting transfers between devices, by_batch(): lax.all_to_all(piece, ('idx', 'half'), split_axis=0, concat_axis=0, tiled...  27.1 us
    dot_general x6, matrix products, complex_product(): jnp.einsum(pattern, left_real + left_imag, right_real + right_imag, preci...  23.6 us
    dot_general x6, matrix products, complex_product(): first_term = jnp.einsum(pattern, left_real, right_real, precision=HIGH)  20.8 us
    dot_general x6, matrix products, complex_product(): second_term = jnp.einsum(pattern, left_imag, right_imag, precision=HIGH)  18 us
    transpose x2, local copies, waits for them, and re-layouts, by_batch(): got.transpose(1, 2, 3, 0, 4, 5)  14.3 us
  transfers between devices with their start and end apart: 4, of which 4 were waited for; matrix products, arithmetic and copies ran while one was open for 10% of the time, Pallas kernels for 0%

commit v1 on v0

--- a/solution.py
+++ b/solution.py
@@ -6,6 +6,22 @@
 
 HIGH = lax.Precision.HIGH
 CHUNKS = (3, 1)
+
+
+def exchange_in_pairs(x, axis, split, join):
+    ways, here = (lax.axis_size(axis), lax.axis_index(axis))
+    width = x.shape[split] // ways
+    shape = list(x.shape)
+    shape[split] = width
+    height = shape[join]
+    shape[join] = height * ways
+    full = jnp.zeros(shape, x.dtype)
+    for mask in range(ways):
+        part = lax.dynamic_slice_in_dim(x, (here ^ mask) * width, width, axis=split)
+        if mask:
+            part = lax.ppermute(part, axis, [(d, d ^ mask) for d in range(ways)])
+        full = lax.dynamic_update_slice_in_dim(full, part, (here ^ mask) * height, axis=join)
+    return full
 
 
 def swapped(x, axis, bit):
@@ -49,9 +65,7 @@
     start = 0
     for size in sizes:
         piece = blocks[:, :, start : start + size].transpose(1, 0, 2, 3, 4)
-        received.append(
-            lax.all_to_all(piece, ("idx", "half"), split_axis=0, concat_axis=0, tiled=True)
-        )
+        received.append(exchange_in_pairs(piece, ("idx", "half"), 0, 0))
         start += size
     outgoing = lax.dynamic_slice_in_dim(left_local, (1 - half_index) * mine, mine, 1)
     own = lax.dynamic_slice_in_dim(left_local, half_index * mine, mine, 1)

time: 584 us -> 695 us (1.19)
  starting transfers between devices: 27.5 us -> 148 us
  waiting for transfers between devices: 396 us -> 341 us
  local copies, waits for them, and re-layouts: 53.6 us -> 94.5 us
    all_to_all x2 -> x0, waiting for transfers between devices: 235 us -> none  [by_batch(): lax.all_to_all(piece, ('idx', 'half'), split_axis=0, concat_axis=0, tiled...]
    ppermute x0 -> x30, waiting for transfers between devices: none -> 177 us  [exchange_in_pairs(): part = lax.ppermute(part, axis, [(d, d ^ mask) for d in range(ways)])]
    ppermute x0 -> x30, starting transfers between devices: none -> 148 us  [exchange_in_pairs(): part = lax.ppermute(part, axis, [(d, d ^ mask) for d in range(ways)])]
    dynamic_update_slice x0 -> x32, local copies, waits for them, and re-layouts: none -> 32.9 us  [exchange_in_pairs(): lax.dynamic_update_slice_in_dim(full, part, (here ^ mask) * height, axis=...]
    transpose x4 -> x0, local copies, waits for them, and re-layouts: 28.4 us -> none  [by_batch(): piece = blocks[:, :, start:start + size].transpose(1, 0, 2, 3, 4)]
    all_to_all x2 -> x0, starting transfers between devices: 27.1 us -> none  [by_batch(): lax.all_to_all(piece, ('idx', 'half'), split_axis=0, concat_axis=0, tiled...]
    slice x0 -> x2, local copies, waits for them, and re-layouts: none -> 16.7 us  [by_batch(): piece = blocks[:, :, start:start + size].transpose(1, 0, 2, 3, 4)]
    dynamic_slice x0 -> x2, local copies, waits for them, and re-layouts: none -> 12.2 us  [exchange_in_pairs(): part = lax.dynamic_slice_in_dim(x, (here ^ mask) * width, width, axis=split)]
  transfers between devices with their start and end apart: 4 -> 32, of which waited for: 4 -> 13; matrix products, arithmetic and copies ran while one was open for 10% -> 14% of each run, Pallas kernels for 0% -> 0%
where the time goes in v1:
time: 695 us; the launch traced here: 686 us
  waiting for transfers between devices  341 us (49%)
  starting transfers between devices  148 us (21%)
  local copies, waits for them, and re-layouts  94.5 us (14%)
  matrix products  60.5 us (9%)
  other arithmetic  27.5 us (4%)
  between operations  14.2 us (2%)
    ppermute x30, waiting for transfers between devices, exchange_in_pairs(): part = lax.ppermute(part, axis, [(d, d ^ mask) for d in range(ways)])  177 us
    reduce_scatter x1, waiting for transfers between devices, on_device(): lax.psum_scatter(form(left_local, right_local, norm_scale), ('idx', 'half...  164 us
    ppermute x30, starting transfers between devices, exchange_in_pairs(): part = lax.ppermute(part, axis, [(d, d ^ mask) for d in range(ways)])  148 us
    dynamic_update_slice x32, local copies, waits for them, and re-layouts, exchange_in_pairs(): lax.dynamic_update_slice_in_dim(full, part, (here ^ mask) * height, axis=...  32.9 us
    dot_general x6, matrix products, complex_product(): jnp.einsum(pattern, left_real + left_imag, right_real + right_imag, preci...  23.9 us
    dot_general x6, matrix products, complex_product(): first_term = jnp.einsum(pattern, left_real, right_real, precision=HIGH)  18.8 us
    dot_general x6, matrix products, complex_product(): second_term = jnp.einsum(pattern, left_imag, right_imag, precision=HIGH)  17.8 us
    slice x2, local copies, waits for them, and re-layouts, by_batch(): piece = blocks[:, :, start:start + size].transpose(1, 0, 2, 3, 4)  16.7 us
  transfers between devices with their start and end apart: 32, of which 13 were waited for; matrix products, arithmetic and copies ran while one was open for 14% of the time, Pallas kernels for 0%

profile of v1, /device:TPU:0, one launch (start us, length us, event | category | flops | bytes accessed | tf_op | source)
XLA Modules:
  0.0 685.9 jit_solution(4111905878539965840)
XLA Ops:
  6.5 7.2 %dynamic-slice_bitcast_fusion = f32[2,4,1024,256]{3,2,1,0:T(8,128)} fusion(f32[1,2,8,1024,256]{4,3,2,1,0:T(8,128)} %param.2, s32[]{:T(128)S(6)} %select_n.48), kind=kLoop, calls=%fused_computation.3 | loop fusion | bytes 16777220 | tf_op jit(solution)/shard_map/dynamic_slice | solution.py:70
  27.5 11.9 %slice.85 = f32[2,16,3,32,1024]{4,3,2,1,0:T(8,128)} slice(f32[2,16,4,32,1024]{4,3,2,1,0:T(8,128)} %bitcast.285), slice={[0:2], [0:16], [0:3], [0:32], [0:1024]} | slice | bytes 25165824 | tf_op jit(solution)/shard_map/slice | solution.py:67
  39.4 8.2 %dynamic-slice_bitcast_fusion.1 = (f32[1,2,3,32,1024]{4,3,2,1,0:T(8,128)S(1)}, f32[1,2,3,32,1024]{4,3,2,1,0:T(8,128)S(1)}, f32[1,2,3,32,1024]{4,3,2,1,0:T(8,128)...) fusion(f32[2,16,3,32,1024]{4,3,2,1,0:T(8,128)} %slice.85, ...), kind=kLoop, calls=%fused_computation.84 | loop fusion | bytes 23593020 | tf_op jit(solution)/shard_map/dynamic_slice | solution.py:20
  47.6 6.2 broadcast_in_dim.6
  72.7 14.6 %collective-permute-done.21 = f32[1,2,1,32,1024]{4,3,1,0,2:T(8,128)S(1)} collective-permute-done((f32[1,2,1,32,1024]{4,3,1,0,2:T(8,128)}, f32[1,2,1,32,1024]{4,3,1,0,2:T(8,128)S(1)}, u32[]{:S(2)}, u32[]{:S(2)}) %collective-permute-start.21) | collective-permute-done | bytes 262176 | tf_op jit(solution)/shard_map/ppermute | solution.py:22
  94.8 18.6 %collective-permute-start.28 = (f32[1,2,1,32,1024]{4,3,1,0,2:T(8,128)}, f32[1,2,1,32,1024]{4,3,1,0,2:T(8,128)S(1)}, u32[]{:S(2)}, u32[]{:S(2)}) collective-permute-start(f32[1,2,1,32,1024]{4,3,1,0,2:T(8,128)} %get-tuple-element.24), channel_id=1, source_target_pairs={{0,13},{1,12},{2,15},{3,14},{4,9},{5,8},{6,11},{7,10},{8,5},{9,4},... | collective-permute-start | bytes 786440 | tf_op jit(solution)/shard_map/ppermute | solution.py:22
  113.4 9.1 %collective-permute-done.25 = f32[1,2,1,32,1024]{4,3,1,0,2:T(8,128)S(1)} collective-permute-done((f32[1,2,1,32,1024]{4,3,1,0,2:T(8,128)}, f32[1,2,1,32,1024]{4,3,1,0,2:T(8,128)S(1)}, u32[]{:S(2)}, u32[]{:S(2)}) %collective-permute-start.25) | collective-permute-done | bytes 262176 | tf_op jit(solution)/shard_map/ppermute | solution.py:22
  147.2 19.1 %collective-permute-start.4 = (f32[1,2,3,32,1024]{4,3,2,1,0:T(8,128)S(1)}, f32[1,2,3,32,1024]{4,3,2,1,0:T(8,128)S(1)}, u32[]{:S(2)}, u32[]{:S(2)}) collective-permute-start(f32[1,2,3,32,1024]{4,3,2,1,0:T(8,128)S(1)} %copy-done.9), channel_id=1, source_target_pairs={{0,4},{1,5},{2,6},{3,7},{4,0},{5,1},{6,2},{7,3},{8,12},{9,13},{10,... | collective-permute-start | bytes 2359304 | tf_op jit(solution)/shard_map/ppermute | solution.py:22
  174.0 13.3 %collective-permute-start.7 = (f32[1,2,3,32,1024]{4,3,2,1,0:T(8,128)S(1)}, f32[1,2,3,32,1024]{4,3,2,1,0:T(8,128)S(1)}, u32[]{:S(2)}, u32[]{:S(2)}) collective-permute-start(f32[1,2,3,32,1024]{4,3,2,1,0:T(8,128)S(1)} %copy-done.6), channel_id=1, source_target_pairs={{0,7},{1,6},{2,5},{3,4},{4,3},{5,2},{6,1},{7,0},{8,15},{9,14},{10,... | collective-permute-start | bytes 2359304 | tf_op jit(solution)/shard_map/ppermute | solution.py:22
  189.4 27.6 %collective-permute-done.5 = f32[1,2,3,32,1024]{4,3,2,1,0:T(8,128)S(1)} collective-permute-done((f32[1,2,3,32,1024]{4,3,2,1,0:T(8,128)S(1)}, f32[1,2,3,32,1024]{4,3,2,1,0:T(8,128)S(1)}, u32[]{:S(2)}, u32[]{:S(2)}) %collective-permute-start.5) | collective-permute-done | bytes 786464 | tf_op jit(solution)/shard_map/ppermute | solution.py:22
  219.4 32.4 %collective-permute-done.6 = f32[1,2,3,32,1024]{4,3,2,1,0:T(8,128)S(1)} collective-permute-done((f32[1,2,3,32,1024]{4,3,2,1,0:T(8,128)S(1)}, f32[1,2,3,32,1024]{4,3,2,1,0:T(8,128)S(1)}, u32[]{:S(2)}, u32[]{:S(2)}) %collective-permute-start.6) | collective-permute-done | bytes 786464 | tf_op jit(solution)/shard_map/ppermute | solution.py:22
  252.7 14.7 %collective-permute-done.7 = f32[1,2,3,32,1024]{4,3,2,1,0:T(8,128)S(1)} collective-permute-done((f32[1,2,3,32,1024]{4,3,2,1,0:T(8,128)S(1)}, f32[1,2,3,32,1024]{4,3,2,1,0:T(8,128)S(1)}, u32[]{:S(2)}, u32[]{:S(2)}) %collective-permute-start.7) | collective-permute-done | bytes 786464 | tf_op jit(solution)/shard_map/ppermute | solution.py:22
  272.9 54.0 %collective-permute-start.13 = (f32[1,2,3,32,1024]{4,3,2,1,0:T(8,128)S(1)}, f32[1,2,3,32,1024]{4,3,2,1,0:T(8,128)S(1)}, u32[]{:S(2)}, u32[]{:S(2)}) collective-permute-start(f32[1,2,3,32,1024]{4,3,2,1,0:T(8,128)S(1)} %get-tuple-element.9), channel_id=1, source_target_pairs={{0,13},{1,12},{2,15},{3,14},{4,9},{5,8},{6,11},{7,10},{8,5},{9,4},... | collective-permute-start | bytes 2359304 | tf_op jit(solution)/shard_map/ppermute | solution.py:22
  327.9 28.6 %collective-permute-done.10 = f32[1,2,3,32,1024]{4,3,2,1,0:T(8,128)S(1)} collective-permute-done((f32[1,2,3,32,1024]{4,3,2,1,0:T(8,128)S(1)}, f32[1,2,3,32,1024]{4,3,2,1,0:T(8,128)S(1)}, u32[]{:S(2)}, u32[]{:S(2)}) %collective-permute-start.10) | collective-permute-done | bytes 786464 | tf_op jit(solution)/shard_map/ppermute | solution.py:22
  362.7 26.6 %collective-permute-done.11 = f32[1,2,3,32,1024]{4,3,2,1,0:T(8,128)S(1)} collective-permute-done((f32[1,2,3,32,1024]{4,3,2,1,0:T(8,128)S(1)}, f32[1,2,3,32,1024]{4,3,2,1,0:T(8,128)S(1)}, u32[]{:S(2)}, u32[]{:S(2)}) %collective-permute-start.11) | collective-permute-done | bytes 786464 | tf_op jit(solution)/shard_map/ppermute | solution.py:22
  400.6 12.2 %collective-permute-done.15 = f32[1,2,3,32,1024]{4,3,2,1,0:T(8,128)S(1)} collective-permute-done((f32[1,2,3,32,1024]{4,3,2,1,0:T(8,128)S(1)}, f32[1,2,3,32,1024]{4,3,2,1,0:T(8,128)S(1)}, u32[]{:S(2)}, u32[]{:S(2)}) %collective-permute-start.15) | collective-permute-done | bytes 786464 | tf_op jit(solution)/shard_map/ppermute | solution.py:22
  413.8 12.0 %copy.8 = f32[2,2,3,8,32,1024]{5,4,3,2,1,0:T(8,128)} copy(f32[2,2,3,8,32,1024]{5,4,2,1,0,3:T(8,128)} %bitcast.21) | data formatting | bytes 25165824 | tf_op jit(solution)/shard_map/transpose | solution.py:80
  437.4 10.0 %bitcast_select_fusion = (f32[2,4,1024,256]{3,2,1,0:T(8,128)}, f32[2,4,1024,256]{3,2,1,0:T(8,128)S(1)}) fusion(f32[2,4,1024,256]{3,2,1,0:T(8,128)} %collective-permute-done, f32[1,2,8,1024,256]{4,3,2,1,0:T(8,128)} %param.2, s32[]{:T(128)S(6)} %select_n.47, pred[]{:T(512)S(6)} %eq.3), kind=kLoop, calls=%fused_computation.1 | loop fusion | flops 4194304 | bytes 33554436 | tf_op jit(solution)/shard_map/jit(_where)/select_n | solution.py:75
  454.5 9.0 %fusion.17 = f32[1024,1024,1]{1,0,2:T(8,128)} fusion(f32[2,4,1024,256]{3,2,1,0:T(8,128)} %get-tuple-element.5, f32[3,1024,256]{2,1,0:T(8,128)S(1)} %fusion.13, f32[3,1024,256]{2,1,0:T(8,128)S(1)} %fusion.16), kind=kOutput, calls=%fused_computation.32 | convolution fusion | flops 4832624640 | bytes 13631488 | tf_op jit(solution)/shard_map/bml,bol->mo/dot_general | solution.py:32
  474.4 6.8 fusion.18
  481.1 8.7 %fusion.4 = f32[1024,1,1024]{2,0,1:T(8,128)} fusion(f32[1024,1024,1]{1,0,2:T(8,128)} %fusion.18, f32[1024,1024,1]{1,0,2:T(8,128)} %fusion.17, f32[1024,1024]{1,0:T(8,128)S(1)} %fusion.44, f32[1024,1024]{1,0:T(8,128)} %fusion.41), kind=kLoop, calls=%fused_computation.10 | loop fusion | flops 3145728 | bytes 20971520 | tf_op jit(solution)/shard_map/stack | solution.py:88
  489.8 13.5 %fusion.2 = f32[1024,1,1024]{2,0,1:T(8,128)} fusion(f32[1024,1024,1]{1,0,2:T(8,128)} %fusion.18, f32[1024,1024,1]{1,0,2:T(8,128)} %fusion.17, f32[1024,1024]{1,0:T(8,128)} %fusion.41, f32[1024,1024]{1,0:T(8,128)} %fusion.39, f32[1024,1024]{1,0:T(8,128)S(1)} %fusion.44, f32[2,4,1024,256]{3,2,1,0:T(8,128)} %get-tuple-element.5, ...), kind=kOutput, calls=%fused_computation.7 | convolution fusion | flops 4839440384 | bytes 40894464 | tf_op jit(solution)/shard_map/bml,bol->mo/dot_general | solution.py:34
  503.4 8.8 %maximum_multiply_fusion = f32[1024,2,1024]{2,0,1:T(8,128)} fusion(f32[1024,1,1024]{2,0,1:T(8,128)} %fusion.2, f32[1024,1,1024]{2,0,1:T(8,128)} %fusion.4), kind=kLoop, calls=%fused_computation | loop fusion | flops 4194304 | bytes 16777216 | tf_op jit(solution)/shard_map/mul | solution.py:88
  512.2 164.2 %reduce-scatter.2.cloned.1.call-done = f32[64,2,1024]{2,0,1:T(8,128)} async-done(((f32[1024,2,1024]{2,0,1:T(8,128)}), f32[64,2,1024]{2,0,1:T(8,128)}) %reduce-scatter.2.cloned.1.call-update) | async-done | bytes 524304 | tf_op jit(solution)/shard_map/reduce_scatter | solution.py:98
  (135 shorter events, 134.4 us)
Async XLA Ops:
  6.5 669.8 %reduce-scatter.2.cloned.1.call-start = ((), (), s32[]{:S(2)}) async-start(), calls=%async_computation.1 | async-start | bytes 8912896 | tf_op jit(solution)/shard_map/reduce_scatter | solution.py:98
  13.7 423.7 %collective-permute-start = (f32[2,4,1024,256]{3,2,1,0:T(8,128)}, f32[2,4,1024,256]{3,2,1,0:T(8,128)}, u32[]{:S(2)}, u32[]{:S(2)}) collective-permute-start(f32[2,4,1024,256]{3,2,1,0:T(8,128)} %dynamic-slice_bitcast_fusion), channel_id=1, source_target_pairs={{0,1},{1,0},{2,3},{3,2},{4,5},{5,4},{6,7},{7,6},{8,9},{9,8},{10,11... | collective-permute-start | bytes 25165832 | tf_op jit(solution)/shard_map/ppermute | solution.py:28
  22.9 37.2 %collective-permute-start.16 = (f32[1,2,1,32,1024]{4,3,1,0,2:T(8,128)}, f32[1,2,1,32,1024]{4,3,1,0,2:T(8,128)}, u32[]{:S(2)}, u32[]{:S(2)}) collective-permute-start(f32[1,2,1,32,1024]{4,3,1,0,2:T(8,128)} %get-tuple-element.36), channel_id=1, source_target_pairs={{0,1},{1,0},{2,3},{3,2},{4,5},{5,4},{6,7},{7,6},{8,9},{9,8},{10,11... | collective-permute-start | bytes 786440 | tf_op jit(solution)/shard_map/ppermute | solution.py:22
  23.0 39.3 %collective-permute-start.17 = (f32[1,2,1,32,1024]{4,3,1,0,2:T(8,128)}, f32[1,2,1,32,1024]{4,3,1,0,2:T(8,128)}, u32[]{:S(2)}, u32[]{:S(2)}) collective-permute-start(f32[1,2,1,32,1024]{4,3,1,0,2:T(8,128)} %get-tuple-element.35), channel_id=1, source_target_pairs={{0,2},{1,3},{2,0},{3,1},{4,6},{5,7},{6,4},{7,5},{8,10},{9,11},{10,... | collective-permute-start | bytes 786440 | tf_op jit(solution)/shard_map/ppermute | solution.py:22
  25.9 40.5 %collective-permute-start.18 = (f32[1,2,1,32,1024]{4,3,1,0,2:T(8,128)}, f32[1,2,1,32,1024]{4,3,1,0,2:T(8,128)}, u32[]{:S(2)}, u32[]{:S(2)}) collective-permute-start(f32[1,2,1,32,1024]{4,3,1,0,2:T(8,128)} %get-tuple-element.34), channel_id=1, source_target_pairs={{0,3},{1,2},{2,1},{3,0},{4,7},{5,6},{6,5},{7,4},{8,11},{9,10},{10,... | collective-permute-start | bytes 786440 | tf_op jit(solution)/shard_map/ppermute | solution.py:22
  25.9 40.5 %collective-permute-start.19 = (f32[1,2,1,32,1024]{4,3,1,0,2:T(8,128)}, f32[1,2,1,32,1024]{4,3,1,0,2:T(8,128)}, u32[]{:S(2)}, u32[]{:S(2)}) collective-permute-start(f32[1,2,1,32,1024]{4,3,1,0,2:T(8,128)} %get-tuple-element.33), channel_id=1, source_target_pairs={{0,4},{1,5},{2,6},{3,7},{4,0},{5,1},{6,2},{7,3},{8,12},{9,13},{10,... | collective-permute-start | bytes 786440 | tf_op jit(solution)/shard_map/ppermute | solution.py:22
  87.3 35.2 %collective-permute-start.25 = (f32[1,2,1,32,1024]{4,3,1,0,2:T(8,128)}, f32[1,2,1,32,1024]{4,3,1,0,2:T(8,128)S(1)}, u32[]{:S(2)}, u32[]{:S(2)}) collective-permute-start(f32[1,2,1,32,1024]{4,3,1,0,2:T(8,128)} %get-tuple-element.27), channel_id=1, source_target_pairs={{0,10},{1,11},{2,8},{3,9},{4,14},{5,15},{6,12},{7,13},{8,2},{9,3},... | collective-permute-start | bytes 786440 | tf_op jit(solution)/shard_map/ppermute | solution.py:22
  91.8 36.3 %collective-permute-start.26 = (f32[1,2,1,32,1024]{4,3,1,0,2:T(8,128)}, f32[1,2,1,32,1024]{4,3,1,0,2:T(8,128)S(1)}, u32[]{:S(2)}, u32[]{:S(2)}) collective-permute-start(f32[1,2,1,32,1024]{4,3,1,0,2:T(8,128)} %get-tuple-element.26), channel_id=1, source_target_pairs={{0,11},{1,10},{2,9},{3,8},{4,15},{5,14},{6,13},{7,12},{8,3},{9,2},... | collective-permute-start | bytes 786440 | tf_op jit(solution)/shard_map/ppermute | solution.py:22
  91.8 36.4 %collective-permute-start.27 = (f32[1,2,1,32,1024]{4,3,1,0,2:T(8,128)}, f32[1,2,1,32,1024]{4,3,1,0,2:T(8,128)S(1)}, u32[]{:S(2)}, u32[]{:S(2)}) collective-permute-start(f32[1,2,1,32,1024]{4,3,1,0,2:T(8,128)} %get-tuple-element.25), channel_id=1, source_target_pairs={{0,12},{1,13},{2,14},{3,15},{4,8},{5,9},{6,10},{7,11},{8,4},{9,5},... | collective-permute-start | bytes 786440 | tf_op jit(solution)/shard_map/ppermute | solution.py:22
  94.8 41.0 %collective-permute-start.28 = (f32[1,2,1,32,1024]{4,3,1,0,2:T(8,128)}, f32[1,2,1,32,1024]{4,3,1,0,2:T(8,128)S(1)}, u32[]{:S(2)}, u32[]{:S(2)}) collective-permute-start(f32[1,2,1,32,1024]{4,3,1,0,2:T(8,128)} %get-tuple-element.24), channel_id=1, source_target_pairs={{0,13},{1,12},{2,15},{3,14},{4,9},{5,8},{6,11},{7,10},{8,5},{9,4},... | collective-permute-start | bytes 786440 | tf_op jit(solution)/shard_map/ppermute | solution.py:22
  128.1 42.3 %collective-permute-start.1 = (f32[1,2,3,32,1024]{4,3,2,1,0:T(8,128)S(1)}, f32[1,2,3,32,1024]{4,3,2,1,0:T(8,128)S(1)}, u32[]{:S(2)}, u32[]{:S(2)}) collective-permute-start(f32[1,2,3,32,1024]{4,3,2,1,0:T(8,128)S(1)} %copy-done.12), channel_id=1, source_target_pairs={{0,1},{1,0},{2,3},{3,2},{4,5},{5,4},{6,7},{7,6},{8,9},{9,8},{10,11... | collective-permute-start | bytes 2359304 | tf_op jit(solution)/shard_map/ppermute | solution.py:22
  128.2 42.3 %collective-permute-start.2 = (f32[1,2,3,32,1024]{4,3,2,1,0:T(8,128)S(1)}, f32[1,2,3,32,1024]{4,3,2,1,0:T(8,128)S(1)}, u32[]{:S(2)}, u32[]{:S(2)}) collective-permute-start(f32[1,2,3,32,1024]{4,3,2,1,0:T(8,128)S(1)} %copy-done.11), channel_id=1, source_target_pairs={{0,2},{1,3},{2,0},{3,1},{4,6},{5,7},{6,4},{7,5},{8,10},{9,11},{10,... | collective-permute-start | bytes 2359304 | tf_op jit(solution)/shard_map/ppermute | solution.py:22
  135.8 38.2 %collective-permute-start.3 = (f32[1,2,3,32,1024]{4,3,2,1,0:T(8,128)S(1)}, f32[1,2,3,32,1024]{4,3,2,1,0:T(8,128)S(1)}, u32[]{:S(2)}, u32[]{:S(2)}) collective-permute-start(f32[1,2,3,32,1024]{4,3,2,1,0:T(8,128)S(1)} %copy-done.10), channel_id=1, source_target_pairs={{0,3},{1,2},{2,1},{3,0},{4,7},{5,6},{6,5},{7,4},{8,11},{9,10},{10,... | collective-permute-start | bytes 2359304 | tf_op jit(solution)/shard_map/ppermute | solution.py:22
  147.2 40.7 %collective-permute-start.4 = (f32[1,2,3,32,1024]{4,3,2,1,0:T(8,128)S(1)}, f32[1,2,3,32,1024]{4,3,2,1,0:T(8,128)S(1)}, u32[]{:S(2)}, u32[]{:S(2)}) collective-permute-start(f32[1,2,3,32,1024]{4,3,2,1,0:T(8,128)S(1)} %copy-done.9), channel_id=1, source_target_pairs={{0,4},{1,5},{2,6},{3,7},{4,0},{5,1},{6,2},{7,3},{8,12},{9,13},{10,... | collective-permute-start | bytes 2359304 | tf_op jit(solution)/shard_map/ppermute | solution.py:22
  170.4 46.7 %collective-permute-start.5 = (f32[1,2,3,32,1024]{4,3,2,1,0:T(8,128)S(1)}, f32[1,2,3,32,1024]{4,3,2,1,0:T(8,128)S(1)}, u32[]{:S(2)}, u32[]{:S(2)}) collective-permute-start(f32[1,2,3,32,1024]{4,3,2,1,0:T(8,128)S(1)} %copy-done.8), channel_id=1, source_target_pairs={{0,5},{1,4},{2,7},{3,6},{4,1},{5,0},{6,3},{7,2},{8,13},{9,12},{10,... | collective-permute-start | bytes 2359304 | tf_op jit(solution)/shard_map/ppermute | solution.py:22
  170.5 81.2 %collective-permute-start.6 = (f32[1,2,3,32,1024]{4,3,2,1,0:T(8,128)S(1)}, f32[1,2,3,32,1024]{4,3,2,1,0:T(8,128)S(1)}, u32[]{:S(2)}, u32[]{:S(2)}) collective-permute-start(f32[1,2,3,32,1024]{4,3,2,1,0:T(8,128)S(1)} %copy-done.7), channel_id=1, source_target_pairs={{0,6},{1,7},{2,4},{3,5},{4,2},{5,3},{6,0},{7,1},{8,14},{9,15},{10,... | collective-permute-start | bytes 2359304 | tf_op jit(solution)/shard_map/ppermute | solution.py:22
  174.0 93.5 %collective-permute-start.7 = (f32[1,2,3,32,1024]{4,3,2,1,0:T(8,128)S(1)}, f32[1,2,3,32,1024]{4,3,2,1,0:T(8,128)S(1)}, u32[]{:S(2)}, u32[]{:S(2)}) collective-permute-start(f32[1,2,3,32,1024]{4,3,2,1,0:T(8,128)S(1)} %copy-done.6), channel_id=1, source_target_pairs={{0,7},{1,6},{2,5},{3,4},{4,3},{5,2},{6,1},{7,0},{8,15},{9,14},{10,... | collective-permute-start | bytes 2359304 | tf_op jit(solution)/shard_map/ppermute | solution.py:22
  187.9 82.4 %collective-permute-start.8 = (f32[1,2,3,32,1024]{4,3,2,1,0:T(8,128)S(1)}, f32[1,2,3,32,1024]{4,3,2,1,0:T(8,128)S(1)}, u32[]{:S(2)}, u32[]{:S(2)}) collective-permute-start(f32[1,2,3,32,1024]{4,3,2,1,0:T(8,128)S(1)} %copy-done.5), channel_id=1, source_target_pairs={{0,8},{1,9},{2,10},{3,11},{4,12},{5,13},{6,14},{7,15},{8,0},{9,1},... | collective-permute-start | bytes 2359304 | tf_op jit(solution)/shard_map/ppermute | solution.py:22
  217.1 55.8 %collective-permute-start.9 = (f32[1,2,3,32,1024]{4,3,2,1,0:T(8,128)S(1)}, f32[1,2,3,32,1024]{4,3,2,1,0:T(8,128)S(1)}, u32[]{:S(2)}, u32[]{:S(2)}) collective-permute-start(f32[1,2,3,32,1024]{4,3,2,1,0:T(8,128)S(1)} %copy-done.4), channel_id=1, source_target_pairs={{0,9},{1,8},{2,11},{3,10},{4,13},{5,12},{6,15},{7,14},{8,1},{9,0},... | collective-permute-start | bytes 2359304 | tf_op jit(solution)/shard_map/ppermute | solution.py:22
  251.7 104.8 %collective-permute-start.10 = (f32[1,2,3,32,1024]{4,3,2,1,0:T(8,128)S(1)}, f32[1,2,3,32,1024]{4,3,2,1,0:T(8,128)S(1)}, u32[]{:S(2)}, u32[]{:S(2)}) collective-permute-start(f32[1,2,3,32,1024]{4,3,2,1,0:T(8,128)S(1)} %copy-done.3), channel_id=1, source_target_pairs={{0,10},{1,11},{2,8},{3,9},{4,14},{5,15},{6,12},{7,13},{8,2},{9,3},... | collective-permute-start | bytes 2359304 | tf_op jit(solution)/shard_map/ppermute | solution.py:22
  267.4 121.9 %collective-permute-start.11 = (f32[1,2,3,32,1024]{4,3,2,1,0:T(8,128)S(1)}, f32[1,2,3,32,1024]{4,3,2,1,0:T(8,128)S(1)}, u32[]{:S(2)}, u32[]{:S(2)}) collective-permute-start(f32[1,2,3,32,1024]{4,3,2,1,0:T(8,128)S(1)} %copy-done.2), channel_id=1, source_target_pairs={{0,11},{1,10},{2,9},{3,8},{4,15},{5,14},{6,13},{7,12},{8,3},{9,2},... | collective-permute-start | bytes 2359304 | tf_op jit(solution)/shard_map/ppermute | solution.py:22
  270.3 127.5 %collective-permute-start.12 = (f32[1,2,3,32,1024]{4,3,2,1,0:T(8,128)S(1)}, f32[1,2,3,32,1024]{4,3,2,1,0:T(8,128)S(1)}, u32[]{:S(2)}, u32[]{:S(2)}) collective-permute-start(f32[1,2,3,32,1024]{4,3,2,1,0:T(8,128)S(1)} %get-tuple-element.10), channel_id=1, source_target_pairs={{0,12},{1,13},{2,14},{3,15},{4,8},{5,9},{6,10},{7,11},{8,4},{9,5},... | collective-permute-start | bytes 2359304 | tf_op jit(solution)/shard_map/ppermute | solution.py:22
  272.9 125.8 %collective-permute-start.13 = (f32[1,2,3,32,1024]{4,3,2,1,0:T(8,128)S(1)}, f32[1,2,3,32,1024]{4,3,2,1,0:T(8,128)S(1)}, u32[]{:S(2)}, u32[]{:S(2)}) collective-permute-start(f32[1,2,3,32,1024]{4,3,2,1,0:T(8,128)S(1)} %get-tuple-element.9), channel_id=1, source_target_pairs={{0,13},{1,12},{2,15},{3,14},{4,9},{5,8},{6,11},{7,10},{8,5},{9,4},... | collective-permute-start | bytes 2359304 | tf_op jit(solution)/shard_map/ppermute | solution.py:22
  356.5 43.2 %collective-permute-start.14 = (f32[1,2,3,32,1024]{4,3,2,1,0:T(8,128)S(1)}, f32[1,2,3,32,1024]{4,3,2,1,0:T(8,128)S(1)}, u32[]{:S(2)}, u32[]{:S(2)}) collective-permute-start(f32[1,2,3,32,1024]{4,3,2,1,0:T(8,128)S(1)} %get-tuple-element.8), channel_id=1, source_target_pairs={{0,14},{1,15},{2,12},{3,13},{4,10},{5,11},{6,8},{7,9},{8,6},{9,7},... | collective-permute-start | bytes 2359304 | tf_op jit(solution)/shard_map/ppermute | solution.py:22
  (23 other events, 742.4 us)
Sparse Core Ops, SparseCore 0:
  512.3 164.0 reduce-scatter.1
